TPU v7x, 32 devices: a whole 2x2x4 slice. The times are simulated.
32 devices in a mesh: conv: 2 (over y), ctx: 4 (over x, core), head: 4 (over z).
Axes of the slice: x: 2, y: 2, z: 4, core: 2. Of those that a mesh axis runs over, the one named last changes fastest.
Arguments:
- queries: bfloat16 [512, 64, 128], P(('conv', 'ctx'), 'head'), parts along dimension 0, may hold values from -240 to 240, as said below
- new_keys: bfloat16 [512, 8, 128], P(('conv', 'ctx'), 'head'), parts along dimension 0, may hold values from -8 to 8
- new_values: bfloat16 [512, 8, 128], P(('conv', 'ctx'), 'head'), parts along dimension 0, may hold values from -18 to 18
- cache_keys: bfloat16 [16384, 8, 128], P(('conv', 'ctx'), 'head'), parts along dimension 0, may hold values from -6 to 6
- cache_values: bfloat16 [16384, 8, 128], P(('conv', 'ctx'), 'head'), parts along dimension 0, may hold values from -18 to 18
- cache_len: int32 [2], P('conv'), parts along dimension 0, may hold values from 4097 to 8192
Outputs:
- attended: bfloat16 [512, 64, 128], P(('conv', 'ctx'), 'head'), parts along dimension 0
There are 2 independent parts, one for each index of `conv`. A program takes and returns all parts, laid end to end along the dimension named above; each array names one. Nothing has to cross between parts.
Inputs may be any that keep to these rules, and one draw needn't show every extreme that they name: `queries`: each query row is a row of independent entries times a row scale.
All inputs are finite; a program needn't handle non-finite values.
Results may differ from a plain program's by a relative error of at most 0.01.
Values may be sent and summed in bfloat16 or wider, within the bound.
A program may use at most 64 MiB of HBM per device.

v0:
```python
import math
import jax
import jax.numpy as jnp
from jax import lax
from jax.sharding import PartitionSpec as P

NEG_FILL = -1e30


def attend_block(query_rows, keys, values, valid):
    scores = jnp.einsum("tkgd,skd->tkgs", query_rows, keys, preferred_element_type=jnp.float32) * (
        1.0 / math.sqrt(keys.shape[-1])
    )
    mask = valid[:, None, None, :]
    scores = jnp.where(mask, scores, NEG_FILL)
    peak = jnp.max(scores, axis=-1)
    expo = jnp.where(mask, jnp.exp(scores - peak[..., None]), 0.0)
    total = jnp.sum(expo, axis=-1)
    out = jnp.einsum(
        "tkgs,skd->tkgd", expo.astype(jnp.bfloat16), values, preferred_element_type=jnp.float32
    )
    return (out, peak, total)


def per_device(queries, new_keys, new_values, cache_keys, cache_values, cache_len):
    q_rows, heads_local, head_size = queries.shape
    slots, kv_local, _ = cache_keys.shape
    group = heads_local // kv_local
    place = lax.axis_index("ctx")
    limit = cache_len[0]
    slot_valid = place * slots + lax.iota(jnp.int32, slots) < limit
    piece = lax.all_gather(queries, "ctx", axis=0, tiled=True)
    rows = piece.shape[0]
    block = math.gcd(rows, 64)
    blocks = piece.reshape(rows // block, block, kv_local, group, head_size)

    def one_block(blk):
        out, peak, total = attend_block(blk, cache_keys, cache_values, slot_valid[None, :])
        floored = jnp.maximum(total, 1.0)
        norm = (out / floored[..., None]).astype(jnp.bfloat16)
        lse = peak + jnp.log(floored)
        return (norm.reshape(block, heads_local, head_size), lse.reshape(block, heads_local))

    norm, lse = lax.map(one_block, blocks)
    norm, lse = (norm.reshape(rows, heads_local, head_size), lse.reshape(rows, heads_local))
    turn_k, turn_v = (
        lax.all_gather(new_keys, "ctx", axis=0, tiled=True),
        lax.all_gather(new_values, "ctx", axis=0, tiled=True),
    )
    own_ids = place * q_rows + lax.iota(jnp.int32, q_rows)
    causal = lax.iota(jnp.int32, turn_k.shape[0])[None, :] <= own_ids[:, None]
    turn_out, turn_max, turn_total = attend_block(
        queries.reshape(q_rows, kv_local, group, head_size), turn_k, turn_v, causal
    )
    turn_out = turn_out.reshape(q_rows, heads_local, head_size)
    turn_max = turn_max.reshape(q_rows, heads_local)
    turn_total = turn_total.reshape(q_rows, heads_local)
    got_norm = lax.all_to_all(norm[None], "ctx", split_axis=1, concat_axis=0, tiled=True)
    got_lse = lax.all_to_all(lse[None], "ctx", split_axis=1, concat_axis=0, tiled=True)
    top = jnp.maximum(jnp.max(got_lse, axis=0), turn_max)
    shard_scale = jnp.exp(got_lse - top[None])
    numer = jnp.einsum("sthd,sth->thd", got_norm.astype(jnp.float32), shard_scale)
    denom = jnp.sum(shard_scale, axis=0)
    turn_scale = jnp.exp(turn_max - top)
    numer = numer + turn_out * turn_scale[..., None]
    denom = denom + turn_total * turn_scale
    return (numer / denom[..., None]).astype(jnp.bfloat16)


def solution(mesh):
    return jax.shard_map(
        per_device,
        mesh=mesh,
        in_specs=(
            P(("conv", "ctx"), "head", None),
            P(("conv", "ctx"), "head", None),
            P(("conv", "ctx"), "head", None),
            P(("conv", "ctx"), "head", None),
            P(("conv", "ctx"), "head", None),
            P("conv"),
        ),
        out_specs=P(("conv", "ctx"), "head", None),
        check_vma=False,
    )
```

profile of v0, /device:TPU:0, one launch (start us, length us, event | category | flops | bytes accessed | tf_op | source)
XLA Modules:
  0.0 124.3 jit_solution(1532145493059581780)
XLA Ops:
  6.5 0.7 all-gather.2.cloned.1.call-update
  7.3 1.4 %copy.96 = bf16[2048,2,128]{2,0,1:T(8,128)(2,1)S(1)} copy(bf16[2048,2,128]{2,1,0:T(2,128)(2,1)} %param.11) | data formatting | bytes 2097152
  8.7 1.4 %copy.97 = bf16[2048,2,128]{2,0,1:T(8,128)(2,1)S(1)} copy(bf16[2048,2,128]{2,1,0:T(2,128)(2,1)} %param.12) | data formatting | bytes 2097152
  10.0 0.8 copy.100
  10.8 0.8 copy.104
  11.5 6.5 %all_gather.10 = bf16[256,2,128]{2,0,1:T(8,128)(2,1)S(1)} all-gather(bf16[64,2,128]{2,0,1:T(8,128)(2,1)S(1)} %copy.100), channel_id=1, replica_groups=mesh['conv'=2,'ctx'=4,'head'=4] {'ctx'}, dimensions={0}, use_global_device_ids=true | all-gather | bytes 163840 | tf_op jit(solution)/shard_map/all_gather | solution.py:47
  18.0 6.3 %all_gather.11 = bf16[256,2,128]{2,0,1:T(8,128)(2,1)S(1)} all-gather(bf16[64,2,128]{2,0,1:T(8,128)(2,1)S(1)} %copy.104), channel_id=1, replica_groups=mesh['conv'=2,'ctx'=4,'head'=4] {'ctx'}, dimensions={0}, use_global_device_ids=true | all-gather | bytes 163840 | tf_op jit(solution)/shard_map/all_gather | solution.py:48
  24.4 1.3 %fusion.47 = (f32[64,2,8]{0,2,1:T(8,128)S(1)}, f32[64,2,8,256]{3,0,2,1:T(8,128)S(1)}) fusion(bf16[64,2,8,128]{3,2,1,0:T(8,128)(2,1)} %bitcast.124, bf16[256,2,128]{2,0,1:T(8,128)(2,1)S(1)} %all_gather.10, pred[64,256]{1,0:T(8,128)(4,1)S(1)} %iota_compare_fusion), kind=kOutput, calls=%fused_computation.53 | convolution fusion | flops 67894272 | bytes 1462272 | tf_op jit(solution)/shard_map/tkgd,skd->tkgs/dot_general | solution.py:11
  25.8 0.4 fusion.33
  26.2 2.8 %all-gather.2.cloned.1.call-done = bf16[256,16,128]{2,1,0:T(8,128)(2,1)} async-done(((bf16[64,16,128]{2,1,0:T(8,128)(2,1)}), bf16[256,16,128]{2,1,0:T(8,128)(2,1)}) %all-gather.2.cloned.1.call-update) | async-done | bytes 1048592 | tf_op jit(solution)/shard_map/all_gather | solution.py:32
  29.0 58.6 %while.13 = (s32[]{:T(128)}, bf16[4,64,16,128]{3,2,1,0:T(8,128)(2,1)}, f32[4,64,16]{1,2,0:T(8,128)S(1)}, bf16[4,64,2,8,128]{4,3,2,1,0:T(8,128)(2,1)}, bf16[2048,...) while((s32[]{:T(128)}, ...), condition=%wide.region_3.4_spmd.clone, body=%wide.region_0.3_spmd.clone.sunk | while | flops 1101272064 | bytes 61953156 | solution.py:44
  29.0 0.7 add_compare_fusion.2
  29.7 2.4 %bitcast_reduce_fusion.2 = (f32[64,2,8]{2,0,1:T(8,128)S(1)}, f32[2,64,8,2048]{3,2,1,0:T(8,128)S(1)}) fusion(pred[2048]{0:T(1024)(128)(4,1)S(1)} %add_compare_fusion.2, bf16[2048,2,128]{2,0,1:T(8,128)(2,1)S(1)} %get-tuple-element.220, bf16[4,64,2,8,128]{4,3,2,1,0:T(8,128)(2,1)} %get-tuple-element.219, s32[]{:T(128)} %get-tuple-element.207), kind=kOutput, calls=%fused_computation.2.clone.1 | convolution fusion | flops 543161344 | bytes 9705984 | tf_op jit(solution)/shard_map/while/body/eval_jaxpr/tkgd,skd->tkgs/dot_general | solution.py:11
  32.1 3.2 %copy-done = f32[2,64,8,2048]{3,2,1,0:T(8,128)} copy-done((f32[2,64,8,2048]{3,2,1,0:T(8,128)}, f32[2,64,8,2048]{3,2,1,0:T(8,128)S(1)}, u32[]{:S(2)}) %copy-start) | copy-done | bytes 8388632 | tf_op jit(solution)/shard_map/while
  35.4 2.2 %fusion.55 = f32[64,2,8]{2,0,1:T(8,128)S(1)} fusion(f32[2,64,8,2048]{3,2,1,0:T(8,128)S(1)} %get-tuple-element.196, f32[64,2,8]{2,0,1:T(8,128)S(1)} %get-tuple-element.197, pred[2048]{0:T(1024)(128)(4,1)S(1)} %add_compare_fusion.2), kind=kLoop, calls=%fused_computation.6.clone.1 | loop fusion | flops 10484736 | bytes 8398848 | tf_op jit(solution)/shard_map/while/body/eval_jaxpr/reduce_sum | solution.py:18
  37.8 5.1 %fusion.56 = bf16[64,2,8,128]{3,2,0,1:T(8,128)(2,1)S(1)} fusion(bf16[2048,2,128]{2,0,1:T(8,128)(2,1)S(1)} %get-tuple-element.221, f32[2,64,8,2048]{3,2,1,0:T(8,128)} %copy-done, f32[64,2,8]{2,0,1:T(8,128)S(1)} %get-tuple-element.197, pred[2048]{0:T(1024)(128)(4,1)S(1)} %add_compare_fusion.2, f32[64,2,8]{2,0,1:T(8,128)S(1)} %copy.142), kind=kOutput, calls=%fused_computation.16.clone.1 | convolution fusion | flops 547618816 | bytes 9709568 | tf_op jit(solution)/shard_map/while/body/eval_jaxpr/tkgs,skd->tkgd/dot_general | solution.py:19
  42.9 0.8 bitcast_dynamic-update-slice_fusion.4
  43.7 0.7 add_compare_fusion.2
  44.3 2.4 %bitcast_reduce_fusion.2 = (f32[64,2,8]{2,0,1:T(8,128)S(1)}, f32[2,64,8,2048]{3,2,1,0:T(8,128)S(1)}) fusion(pred[2048]{0:T(1024)(128)(4,1)S(1)} %add_compare_fusion.2, bf16[2048,2,128]{2,0,1:T(8,128)(2,1)S(1)} %get-tuple-element.220, bf16[4,64,2,8,128]{4,3,2,1,0:T(8,128)(2,1)} %get-tuple-element.219, s32[]{:T(128)} %get-tuple-element.207), kind=kOutput, calls=%fused_computation.2.clone.1 | convolution fusion | flops 543161344 | bytes 9705984 | tf_op jit(solution)/shard_map/while/body/eval_jaxpr/tkgd,skd->tkgs/dot_general | solution.py:11
  46.8 3.2 %copy-done = f32[2,64,8,2048]{3,2,1,0:T(8,128)} copy-done((f32[2,64,8,2048]{3,2,1,0:T(8,128)}, f32[2,64,8,2048]{3,2,1,0:T(8,128)S(1)}, u32[]{:S(2)}) %copy-start) | copy-done | bytes 8388632 | tf_op jit(solution)/shard_map/while
  50.0 2.2 %fusion.55 = f32[64,2,8]{2,0,1:T(8,128)S(1)} fusion(f32[2,64,8,2048]{3,2,1,0:T(8,128)S(1)} %get-tuple-element.196, f32[64,2,8]{2,0,1:T(8,128)S(1)} %get-tuple-element.197, pred[2048]{0:T(1024)(128)(4,1)S(1)} %add_compare_fusion.2), kind=kLoop, calls=%fused_computation.6.clone.1 | loop fusion | flops 10484736 | bytes 8398848 | tf_op jit(solution)/shard_map/while/body/eval_jaxpr/reduce_sum | solution.py:18
  52.5 5.1 %fusion.56 = bf16[64,2,8,128]{3,2,0,1:T(8,128)(2,1)S(1)} fusion(bf16[2048,2,128]{2,0,1:T(8,128)(2,1)S(1)} %get-tuple-element.221, f32[2,64,8,2048]{3,2,1,0:T(8,128)} %copy-done, f32[64,2,8]{2,0,1:T(8,128)S(1)} %get-tuple-element.197, pred[2048]{0:T(1024)(128)(4,1)S(1)} %add_compare_fusion.2, f32[64,2,8]{2,0,1:T(8,128)S(1)} %copy.142), kind=kOutput, calls=%fused_computation.16.clone.1 | convolution fusion | flops 547618816 | bytes 9709568 | tf_op jit(solution)/shard_map/while/body/eval_jaxpr/tkgs,skd->tkgd/dot_general | solution.py:19
  57.6 0.8 bitcast_dynamic-update-slice_fusion.4
  58.3 0.7 add_compare_fusion.2
  59.0 2.4 %bitcast_reduce_fusion.2 = (f32[64,2,8]{2,0,1:T(8,128)S(1)}, f32[2,64,8,2048]{3,2,1,0:T(8,128)S(1)}) fusion(pred[2048]{0:T(1024)(128)(4,1)S(1)} %add_compare_fusion.2, bf16[2048,2,128]{2,0,1:T(8,128)(2,1)S(1)} %get-tuple-element.220, bf16[4,64,2,8,128]{4,3,2,1,0:T(8,128)(2,1)} %get-tuple-element.219, s32[]{:T(128)} %get-tuple-element.207), kind=kOutput, calls=%fused_computation.2.clone.1 | convolution fusion | flops 543161344 | bytes 9705984 | tf_op jit(solution)/shard_map/while/body/eval_jaxpr/tkgd,skd->tkgs/dot_general | solution.py:11
  61.4 3.2 %copy-done = f32[2,64,8,2048]{3,2,1,0:T(8,128)} copy-done((f32[2,64,8,2048]{3,2,1,0:T(8,128)}, f32[2,64,8,2048]{3,2,1,0:T(8,128)S(1)}, u32[]{:S(2)}) %copy-start) | copy-done | bytes 8388632 | tf_op jit(solution)/shard_map/while
  64.7 2.2 %fusion.55 = f32[64,2,8]{2,0,1:T(8,128)S(1)} fusion(f32[2,64,8,2048]{3,2,1,0:T(8,128)S(1)} %get-tuple-element.196, f32[64,2,8]{2,0,1:T(8,128)S(1)} %get-tuple-element.197, pred[2048]{0:T(1024)(128)(4,1)S(1)} %add_compare_fusion.2), kind=kLoop, calls=%fused_computation.6.clone.1 | loop fusion | flops 10484736 | bytes 8398848 | tf_op jit(solution)/shard_map/while/body/eval_jaxpr/reduce_sum | solution.py:18
  67.1 5.1 %fusion.56 = bf16[64,2,8,128]{3,2,0,1:T(8,128)(2,1)S(1)} fusion(bf16[2048,2,128]{2,0,1:T(8,128)(2,1)S(1)} %get-tuple-element.221, f32[2,64,8,2048]{3,2,1,0:T(8,128)} %copy-done, f32[64,2,8]{2,0,1:T(8,128)S(1)} %get-tuple-element.197, pred[2048]{0:T(1024)(128)(4,1)S(1)} %add_compare_fusion.2, f32[64,2,8]{2,0,1:T(8,128)S(1)} %copy.142), kind=kOutput, calls=%fused_computation.16.clone.1 | convolution fusion | flops 547618816 | bytes 9709568 | tf_op jit(solution)/shard_map/while/body/eval_jaxpr/tkgs,skd->tkgd/dot_general | solution.py:19
  72.2 0.8 bitcast_dynamic-update-slice_fusion.4
  73.0 0.7 add_compare_fusion.2
  73.7 2.4 %bitcast_reduce_fusion.2 = (f32[64,2,8]{2,0,1:T(8,128)S(1)}, f32[2,64,8,2048]{3,2,1,0:T(8,128)S(1)}) fusion(pred[2048]{0:T(1024)(128)(4,1)S(1)} %add_compare_fusion.2, bf16[2048,2,128]{2,0,1:T(8,128)(2,1)S(1)} %get-tuple-element.220, bf16[4,64,2,8,128]{4,3,2,1,0:T(8,128)(2,1)} %get-tuple-element.219, s32[]{:T(128)} %get-tuple-element.207), kind=kOutput, calls=%fused_computation.2.clone.1 | convolution fusion | flops 543161344 | bytes 9705984 | tf_op jit(solution)/shard_map/while/body/eval_jaxpr/tkgd,skd->tkgs/dot_general | solution.py:11
  76.1 3.2 %copy-done = f32[2,64,8,2048]{3,2,1,0:T(8,128)} copy-done((f32[2,64,8,2048]{3,2,1,0:T(8,128)}, f32[2,64,8,2048]{3,2,1,0:T(8,128)S(1)}, u32[]{:S(2)}) %copy-start) | copy-done | bytes 8388632 | tf_op jit(solution)/shard_map/while
  79.3 2.2 %fusion.55 = f32[64,2,8]{2,0,1:T(8,128)S(1)} fusion(f32[2,64,8,2048]{3,2,1,0:T(8,128)S(1)} %get-tuple-element.196, f32[64,2,8]{2,0,1:T(8,128)S(1)} %get-tuple-element.197, pred[2048]{0:T(1024)(128)(4,1)S(1)} %add_compare_fusion.2), kind=kLoop, calls=%fused_computation.6.clone.1 | loop fusion | flops 10484736 | bytes 8398848 | tf_op jit(solution)/shard_map/while/body/eval_jaxpr/reduce_sum | solution.py:18
  81.8 5.1 %fusion.56 = bf16[64,2,8,128]{3,2,0,1:T(8,128)(2,1)S(1)} fusion(bf16[2048,2,128]{2,0,1:T(8,128)(2,1)S(1)} %get-tuple-element.221, f32[2,64,8,2048]{3,2,1,0:T(8,128)} %copy-done, f32[64,2,8]{2,0,1:T(8,128)S(1)} %get-tuple-element.197, pred[2048]{0:T(1024)(128)(4,1)S(1)} %add_compare_fusion.2, f32[64,2,8]{2,0,1:T(8,128)S(1)} %copy.142), kind=kOutput, calls=%fused_computation.16.clone.1 | convolution fusion | flops 547618816 | bytes 9709568 | tf_op jit(solution)/shard_map/while/body/eval_jaxpr/tkgs,skd->tkgd/dot_general | solution.py:19
  86.9 0.8 bitcast_dynamic-update-slice_fusion.4
  87.8 0.6 broadcast.66
  88.4 1.0 reduce
  89.4 0.7 reshape.128
  90.1 3.3 %all-to-all-start.1 = ((f32[4,1,1024]{2,1,0:T(1,128)}), f32[4,1,1024]{2,1,0:T(1,128)S(1)}, u32[]{:S(2)}, u32[]{:S(2)}) async-start(f32[4,1,1024]{2,1,0:T(1,128)} %reshape.128), calls=%async_computation.1 | async-start | bytes 32768 | tf_op jit(solution)/shard_map/all_to_all | solution.py:59
  93.4 0.4 convolution_bitcast_fusion
  93.8 3.4 %all-to-all-done.1 = f32[4,1,1024]{2,1,0:T(1,128)S(1)} async-done(((f32[4,1,1024]{2,1,0:T(1,128)}), f32[4,1,1024]{2,1,0:T(1,128)S(1)}, u32[]{:S(2)}, u32[]{:S(2)}) %all-to-all-start.1) | async-done | bytes 16416 | tf_op jit(solution)/shard_map/all_to_all | solution.py:59
  97.2 3.5 %all-to-all-start = ((bf16[1,256,16,128]{3,2,0,1:T(8,128)(2,1)}), bf16[1,256,16,128]{3,2,0,1:T(8,128)(2,1)S(1)}, u32[]{:S(2)}, u32[]{:S(2)}) async-start(bf16[1,256,16,128]{3,2,0,1:T(8,128)(2,1)} %bitcast.2), calls=%async_computation | async-start | bytes 2097152 | tf_op jit(solution)/shard_map/all_to_all | solution.py:58
  100.7 0.7 reduce.1
  101.4 0.2 reshape.129
  102.2 0.7 copy.114
  102.9 12.2 %all-to-all-done = bf16[1,256,16,128]{3,2,0,1:T(8,128)(2,1)S(1)} async-done(((bf16[1,256,16,128]{3,2,0,1:T(8,128)(2,1)}), bf16[1,256,16,128]{3,2,0,1:T(8,128)(2,1)S(1)}, u32[]{:S(2)}, u32[]{:S(2)}) %all-to-all-start) | async-done | bytes 1048608 | tf_op jit(solution)/shard_map/all_to_all | solution.py:58
  115.1 1.3 %fusion.31 = f32[64,16,1,128]{3,2,1,0:T(1,128)S(1)} fusion(bf16[4,64,16,1]{0,3,2,1:T(2,128)(2,1)S(1)} %copy.114, bf16[4,64,16,128]{3,2,1,0:T(8,128)(2,1)S(1)} %bitcast.123), kind=kOutput, calls=%fused_computation.31 | convolution fusion | flops 1048576 | bytes 1581056 | tf_op jit(solution)/shard_map/sthd,sth->thd/dot_general | solution.py:62
  116.4 1.1 fusion.37
  (40 shorter events, 1.6 us)
Async XLA Ops:
  6.5 22.5 %all-gather.2.cloned.1.call-start = ((), (), s32[]{:S(2)}) async-start(), calls=%async_computation.2 | async-start | bytes 1310720 | tf_op jit(solution)/shard_map/all_gather | solution.py:32
  32.1 3.2 %copy-start = (f32[2,64,8,2048]{3,2,1,0:T(8,128)}, f32[2,64,8,2048]{3,2,1,0:T(8,128)S(1)}, u32[]{:S(2)}) copy-start(f32[2,64,8,2048]{3,2,1,0:T(8,128)S(1)} %get-tuple-element.196) | copy-start | bytes 25165828 | tf_op jit(solution)/shard_map/while
  46.8 3.2 %copy-start = (f32[2,64,8,2048]{3,2,1,0:T(8,128)}, f32[2,64,8,2048]{3,2,1,0:T(8,128)S(1)}, u32[]{:S(2)}) copy-start(f32[2,64,8,2048]{3,2,1,0:T(8,128)S(1)} %get-tuple-element.196) | copy-start | bytes 25165828 | tf_op jit(solution)/shard_map/while
  61.4 3.2 %copy-start = (f32[2,64,8,2048]{3,2,1,0:T(8,128)}, f32[2,64,8,2048]{3,2,1,0:T(8,128)S(1)}, u32[]{:S(2)}) copy-start(f32[2,64,8,2048]{3,2,1,0:T(8,128)S(1)} %get-tuple-element.196) | copy-start | bytes 25165828 | tf_op jit(solution)/shard_map/while
  76.1 3.2 %copy-start = (f32[2,64,8,2048]{3,2,1,0:T(8,128)}, f32[2,64,8,2048]{3,2,1,0:T(8,128)S(1)}, u32[]{:S(2)}) copy-start(f32[2,64,8,2048]{3,2,1,0:T(8,128)S(1)} %get-tuple-element.196) | copy-start | bytes 25165828 | tf_op jit(solution)/shard_map/while
  90.1 7.1 %all-to-all-start.1 = ((f32[4,1,1024]{2,1,0:T(1,128)}), f32[4,1,1024]{2,1,0:T(1,128)S(1)}, u32[]{:S(2)}, u32[]{:S(2)}) async-start(f32[4,1,1024]{2,1,0:T(1,128)} %reshape.128), calls=%async_computation.1 | async-start | bytes 32768 | tf_op jit(solution)/shard_map/all_to_all | solution.py:59
  97.2 17.9 %all-to-all-start = ((bf16[1,256,16,128]{3,2,0,1:T(8,128)(2,1)}), bf16[1,256,16,128]{3,2,0,1:T(8,128)(2,1)S(1)}, u32[]{:S(2)}, u32[]{:S(2)}) async-start(bf16[1,256,16,128]{3,2,0,1:T(8,128)(2,1)} %bitcast.2), calls=%async_computation | async-start | bytes 2097152 | tf_op jit(solution)/shard_map/all_to_all | solution.py:58
Sparse Core Ops, SparseCore 0:
  8.9 20.1 all-gather.1
where the time goes:
time: 125 us; the launch traced here: 124 us
  matrix products  33.2 us (27%)
  local copies, waits for them, and re-layouts  23.8 us (19%)
  waiting for transfers between devices  19.2 us (15%)
  other arithmetic  14.9 us (12%)
  between operations  13.5 us (11%)
  blocking collectives  12.8 us (10%)
  starting transfers between devices  6.77 us (5%)
    dot_general x5, matrix products, attend_block(): jnp.einsum('tkgs,skd->tkgd', expo.astype(jnp.bfloat16), values, preferred...  20.8 us
    while x8, local copies, waits for them, and re-layouts  12.9 us
    all_to_all x1, waiting for transfers between devices, per_device(): lax.all_to_all(norm[None], 'ctx', split_axis=1, concat_axis=0, tiled=True)  12.2 us
    dot_general x5, matrix products, attend_block(): jnp.einsum('tkgd,skd->tkgs', query_rows, keys, preferred_element_type=jnp...  11 us
    reduce_sum x5, other arithmetic, attend_block(): total = jnp.sum(expo, axis=-1)  9.28 us
    all_gather x1, blocking collectives, per_device(): lax.all_gather(new_keys, 'ctx', axis=0, tiled=True)  6.49 us
    all_gather x1, blocking collectives, per_device(): lax.all_gather(new_values, 'ctx', axis=0, tiled=True)  6.3 us
    unnamed x7, local copies, waits for them, and re-layouts  5.81 us
  transfers between devices with their start and end apart: 3, of which 3 were waited for; matrix products, arithmetic and copies ran while one was open for 7% of the time, Pallas kernels for 0%

commit v1 on v0

--- a/solution.py
+++ b/solution.py
@@ -5,6 +5,18 @@
 from jax.sharding import PartitionSpec as P
 
 NEG_FILL = -1e30
+
+
+def rotated_exchange(x, axis, split, join):
+    ways, here = (lax.axis_size(axis), lax.axis_index(axis))
+    width = x.shape[split] // ways
+    turned = jnp.roll(x, -here * width, axis=split)
+    got = [lax.slice_in_dim(turned, 0, width, axis=split)]
+    for far in range(1, ways):
+        sent = lax.slice_in_dim(turned, far * width, (far + 1) * width, axis=split)
+        got.append(lax.ppermute(sent, axis, [(d, (d + far) % ways) for d in range(ways)]))
+    line = jnp.concatenate(got[::-1], axis=join)
+    return jnp.roll(line, (here + 1) * got[0].shape[join], axis=join)
 
 
 def attend_block(query_rows, keys, values, valid):
@@ -56,7 +68,7 @@
     turn_max = turn_max.reshape(q_rows, heads_local)
     turn_total = turn_total.reshape(q_rows, heads_local)
     got_norm = lax.all_to_all(norm[None], "ctx", split_axis=1, concat_axis=0, tiled=True)
-    got_lse = lax.all_to_all(lse[None], "ctx", split_axis=1, concat_axis=0, tiled=True)
+    got_lse = rotated_exchange(lse[None], "ctx", 1, 0)
     top = jnp.maximum(jnp.max(got_lse, axis=0), turn_max)
     shard_scale = jnp.exp(got_lse - top[None])
     numer = jnp.einsum("sthd,sth->thd", got_norm.astype(jnp.float32), shard_scale)

time: 125 us -> 118 us (0.944)
  waiting for transfers between devices: 19.2 us -> 17 us
  other arithmetic: 14.9 us -> 13.2 us
  local copies, waits for them, and re-layouts: 23.8 us -> 22.2 us
  starting transfers between devices: 6.77 us -> 5.46 us
    all_to_all x1 -> x0, waiting for transfers between devices: 3.42 us -> none  [per_device(): lax.all_to_all(lse[None], 'ctx', split_axis=1, concat_axis=0, tiled=True)]
    all_to_all x1 -> x0, starting transfers between devices: 3.25 us -> none  [per_device(): lax.all_to_all(lse[None], 'ctx', split_axis=1, concat_axis=0, tiled=True)]
    ppermute x0 -> x3, starting transfers between devices: none -> 1.94 us  [rotated_exchange(): lax.ppermute(sent, axis, [(d, (d + far) % ways) for d in range(ways)])]
    unnamed x7 -> x11, local copies, waits for them, and re-layouts: 5.81 us -> 4.28 us
    dynamic_update_slice x4 -> x8, local copies, waits for them, and re-layouts: 3.06 us -> 3.27 us  [per_device(): norm, lse = lax.map(one_block, blocks)]
  transfers between devices with their start and end apart: 3 -> 5, of which waited for: 3 -> 2; matrix products, arithmetic and copies ran while one was open for 7% -> 6% of each run, Pallas kernels for 0% -> 0%
where the time goes in v1:
time: 118 us
  matrix products  33.1 us (28%)
  local copies, waits for them, and re-layouts  22.2 us (19%)
  waiting for transfers between devices  17 us (14%)
  between operations  13.6 us (12%)
  other arithmetic  13.2 us (11%)
  blocking collectives  12.8 us (11%)
  starting transfers between devices  5.46 us (5%)
    dot_general x5, matrix products, attend_block(): jnp.einsum('tkgs,skd->tkgd', expo.astype(jnp.bfloat16), values, preferred...  20.8 us
    all_to_all x1, waiting for transfers between devices, per_device(): lax.all_to_all(norm[None], 'ctx', split_axis=1, concat_axis=0, tiled=True)  13.4 us
    while x8, local copies, waits for them, and re-layouts  12.9 us
    dot_general x5, matrix products, attend_block(): jnp.einsum('tkgd,skd->tkgs', query_rows, keys, preferred_element_type=jnp...  11 us
    reduce_sum x5, other arithmetic, attend_block(): total = jnp.sum(expo, axis=-1)  9.25 us
    all_gather x1, blocking collectives, per_device(): lax.all_gather(new_keys, 'ctx', axis=0, tiled=True)  6.49 us
    all_gather x1, blocking collectives, per_device(): lax.all_gather(new_values, 'ctx', axis=0, tiled=True)  6.31 us
    unnamed x11, local copies, waits for them, and re-layouts  4.28 us
  transfers between devices with their start and end apart: 5, of which 2 were waited for; matrix products, arithmetic and copies ran while one was open for 6% of the time, Pallas kernels for 0%

profile of v1, /device:TPU:0, one launch (start us, length us, event | category | flops | bytes accessed | tf_op | source)
XLA Modules:
  0.0 117.6 jit_solution(12209949692334802555)
XLA Ops:
  6.5 0.7 all-gather.2.cloned.1.call-update
  7.3 1.4 %copy.61 = bf16[2048,2,128]{2,0,1:T(8,128)(2,1)S(1)} copy(bf16[2048,2,128]{2,1,0:T(2,128)(2,1)} %param.11) | data formatting | bytes 2097152
  8.7 1.4 %copy.62 = bf16[2048,2,128]{2,0,1:T(8,128)(2,1)S(1)} copy(bf16[2048,2,128]{2,1,0:T(2,128)(2,1)} %param.12) | data formatting | bytes 2097152
  10.0 0.8 copy.64
  10.8 0.8 copy.66
  11.6 6.5 %all_gather.10 = bf16[256,2,128]{2,0,1:T(8,128)(2,1)S(1)} all-gather(bf16[64,2,128]{2,0,1:T(8,128)(2,1)S(1)} %copy.64), channel_id=1, replica_groups=mesh['conv'=2,'ctx'=4,'head'=4] {'ctx'}, dimensions={0}, use_global_device_ids=true | all-gather | bytes 163840 | tf_op jit(solution)/shard_map/all_gather | solution.py:59
  18.1 6.3 %all_gather.11 = bf16[256,2,128]{2,0,1:T(8,128)(2,1)S(1)} all-gather(bf16[64,2,128]{2,0,1:T(8,128)(2,1)S(1)} %copy.66), channel_id=1, replica_groups=mesh['conv'=2,'ctx'=4,'head'=4] {'ctx'}, dimensions={0}, use_global_device_ids=true | all-gather | bytes 163840 | tf_op jit(solution)/shard_map/all_gather | solution.py:60
  24.5 1.3 %fusion.49 = (f32[64,2,8]{0,2,1:T(8,128)S(1)}, f32[64,2,8,256]{3,0,2,1:T(8,128)S(1)}) fusion(bf16[64,2,8,128]{3,2,1,0:T(8,128)(2,1)} %bitcast.121, bf16[256,2,128]{2,0,1:T(8,128)(2,1)S(1)} %all_gather.10, pred[64,256]{1,0:T(8,128)(4,1)S(1)} %iota_compare_fusion), kind=kOutput, calls=%fused_computation.66 | convolution fusion | flops 67894272 | bytes 1462272 | tf_op jit(solution)/shard_map/tkgd,skd->tkgs/dot_general | solution.py:23
  25.8 0.4 fusion.33
  26.2 2.8 %all-gather.2.cloned.1.call-done = bf16[256,16,128]{2,1,0:T(8,128)(2,1)} async-done(((bf16[64,16,128]{2,1,0:T(8,128)(2,1)}), bf16[256,16,128]{2,1,0:T(8,128)(2,1)}) %all-gather.2.cloned.1.call-update) | async-done | bytes 1048592 | tf_op jit(solution)/shard_map/all_gather | solution.py:44
  29.0 58.8 %while.13 = (s32[]{:T(128)}, bf16[4,64,16,128]{3,2,1,0:T(8,128)(2,1)}, f32[4,64,16]{1,0,2:T(4,128)S(1)}, bf16[4,64,2,8,128]{4,3,2,1,0:T(8,128)(2,1)}, bf16[2048,...) while((s32[]{:T(128)}, ...), condition=%wide.region_3.4_spmd.clone, body=%wide.region_0.3_spmd.clone.sunk | while | flops 1101271040 | bytes 61944972 | solution.py:56
  29.0 0.7 add_compare_fusion.2
  29.7 2.4 %bitcast_reduce_fusion.2 = (f32[64,2,8]{2,0,1:T(8,128)S(1)}, f32[2,64,8,2048]{3,2,1,0:T(8,128)S(1)}) fusion(pred[2048]{0:T(1024)(128)(4,1)S(1)} %add_compare_fusion.2, bf16[2048,2,128]{2,0,1:T(8,128)(2,1)S(1)} %get-tuple-element.215, bf16[4,64,2,8,128]{4,3,2,1,0:T(8,128)(2,1)} %get-tuple-element.214, s32[]{:T(128)} %get-tuple-element.201), kind=kOutput, calls=%fused_computation.2.clone.1 | convolution fusion | flops 543161344 | bytes 9705984 | tf_op jit(solution)/shard_map/while/body/eval_jaxpr/tkgd,skd->tkgs/dot_general | solution.py:23
  32.1 3.2 %copy-done = f32[2,64,8,2048]{3,2,1,0:T(8,128)} copy-done((f32[2,64,8,2048]{3,2,1,0:T(8,128)}, f32[2,64,8,2048]{3,2,1,0:T(8,128)S(1)}, u32[]{:S(2)}) %copy-start) | copy-done | bytes 8388632 | tf_op jit(solution)/shard_map/while
  35.4 2.2 %fusion.57 = f32[64,2,8]{2,0,1:T(8,128)S(1)} fusion(f32[2,64,8,2048]{3,2,1,0:T(8,128)S(1)} %get-tuple-element.187, f32[64,2,8]{2,0,1:T(8,128)S(1)} %get-tuple-element.188, pred[2048]{0:T(1024)(128)(4,1)S(1)} %add_compare_fusion.2), kind=kLoop, calls=%fused_computation.6.clone.1 | loop fusion | flops 10484736 | bytes 8398848 | tf_op jit(solution)/shard_map/while/body/eval_jaxpr/reduce_sum | solution.py:30
  37.7 0.1 copy.106
  37.8 5.1 %fusion.58 = bf16[64,2,8,128]{3,2,0,1:T(8,128)(2,1)S(1)} fusion(bf16[2048,2,128]{2,0,1:T(8,128)(2,1)S(1)} %get-tuple-element.216, f32[2,64,8,2048]{3,2,1,0:T(8,128)} %copy-done, f32[64,2,8]{2,0,1:T(8,128)S(1)} %get-tuple-element.188, pred[2048]{0:T(1024)(128)(4,1)S(1)} %add_compare_fusion.2, f32[64,2,8]{2,0,1:T(8,128)S(1)} %copy.106), kind=kOutput, calls=%fused_computation.16.clone.1 | convolution fusion | flops 547618816 | bytes 9709568 | tf_op jit(solution)/shard_map/while/body/eval_jaxpr/tkgs,skd->tkgd/dot_general | solution.py:31
  42.9 0.8 bitcast_dynamic-update-slice_fusion.2
  43.7 0.7 add_compare_fusion.2
  44.4 2.4 %bitcast_reduce_fusion.2 = (f32[64,2,8]{2,0,1:T(8,128)S(1)}, f32[2,64,8,2048]{3,2,1,0:T(8,128)S(1)}) fusion(pred[2048]{0:T(1024)(128)(4,1)S(1)} %add_compare_fusion.2, bf16[2048,2,128]{2,0,1:T(8,128)(2,1)S(1)} %get-tuple-element.215, bf16[4,64,2,8,128]{4,3,2,1,0:T(8,128)(2,1)} %get-tuple-element.214, s32[]{:T(128)} %get-tuple-element.201), kind=kOutput, calls=%fused_computation.2.clone.1 | convolution fusion | flops 543161344 | bytes 9705984 | tf_op jit(solution)/shard_map/while/body/eval_jaxpr/tkgd,skd->tkgs/dot_general | solution.py:23
  46.8 3.2 %copy-done = f32[2,64,8,2048]{3,2,1,0:T(8,128)} copy-done((f32[2,64,8,2048]{3,2,1,0:T(8,128)}, f32[2,64,8,2048]{3,2,1,0:T(8,128)S(1)}, u32[]{:S(2)}) %copy-start) | copy-done | bytes 8388632 | tf_op jit(solution)/shard_map/while
  50.0 2.2 %fusion.57 = f32[64,2,8]{2,0,1:T(8,128)S(1)} fusion(f32[2,64,8,2048]{3,2,1,0:T(8,128)S(1)} %get-tuple-element.187, f32[64,2,8]{2,0,1:T(8,128)S(1)} %get-tuple-element.188, pred[2048]{0:T(1024)(128)(4,1)S(1)} %add_compare_fusion.2), kind=kLoop, calls=%fused_computation.6.clone.1 | loop fusion | flops 10484736 | bytes 8398848 | tf_op jit(solution)/shard_map/while/body/eval_jaxpr/reduce_sum | solution.py:30
  52.4 0.1 copy.106
  52.5 5.1 %fusion.58 = bf16[64,2,8,128]{3,2,0,1:T(8,128)(2,1)S(1)} fusion(bf16[2048,2,128]{2,0,1:T(8,128)(2,1)S(1)} %get-tuple-element.216, f32[2,64,8,2048]{3,2,1,0:T(8,128)} %copy-done, f32[64,2,8]{2,0,1:T(8,128)S(1)} %get-tuple-element.188, pred[2048]{0:T(1024)(128)(4,1)S(1)} %add_compare_fusion.2, f32[64,2,8]{2,0,1:T(8,128)S(1)} %copy.106), kind=kOutput, calls=%fused_computation.16.clone.1 | convolution fusion | flops 547618816 | bytes 9709568 | tf_op jit(solution)/shard_map/while/body/eval_jaxpr/tkgs,skd->tkgd/dot_general | solution.py:31
  57.6 0.8 bitcast_dynamic-update-slice_fusion.2
  58.4 0.7 add_compare_fusion.2
  59.1 2.4 %bitcast_reduce_fusion.2 = (f32[64,2,8]{2,0,1:T(8,128)S(1)}, f32[2,64,8,2048]{3,2,1,0:T(8,128)S(1)}) fusion(pred[2048]{0:T(1024)(128)(4,1)S(1)} %add_compare_fusion.2, bf16[2048,2,128]{2,0,1:T(8,128)(2,1)S(1)} %get-tuple-element.215, bf16[4,64,2,8,128]{4,3,2,1,0:T(8,128)(2,1)} %get-tuple-element.214, s32[]{:T(128)} %get-tuple-element.201), kind=kOutput, calls=%fused_computation.2.clone.1 | convolution fusion | flops 543161344 | bytes 9705984 | tf_op jit(solution)/shard_map/while/body/eval_jaxpr/tkgd,skd->tkgs/dot_general | solution.py:23
  61.5 3.2 %copy-done = f32[2,64,8,2048]{3,2,1,0:T(8,128)} copy-done((f32[2,64,8,2048]{3,2,1,0:T(8,128)}, f32[2,64,8,2048]{3,2,1,0:T(8,128)S(1)}, u32[]{:S(2)}) %copy-start) | copy-done | bytes 8388632 | tf_op jit(solution)/shard_map/while
  64.7 2.2 %fusion.57 = f32[64,2,8]{2,0,1:T(8,128)S(1)} fusion(f32[2,64,8,2048]{3,2,1,0:T(8,128)S(1)} %get-tuple-element.187, f32[64,2,8]{2,0,1:T(8,128)S(1)} %get-tuple-element.188, pred[2048]{0:T(1024)(128)(4,1)S(1)} %add_compare_fusion.2), kind=kLoop, calls=%fused_computation.6.clone.1 | loop fusion | flops 10484736 | bytes 8398848 | tf_op jit(solution)/shard_map/while/body/eval_jaxpr/reduce_sum | solution.py:30
  67.1 0.1 copy.106
  67.2 5.1 %fusion.58 = bf16[64,2,8,128]{3,2,0,1:T(8,128)(2,1)S(1)} fusion(bf16[2048,2,128]{2,0,1:T(8,128)(2,1)S(1)} %get-tuple-element.216, f32[2,64,8,2048]{3,2,1,0:T(8,128)} %copy-done, f32[64,2,8]{2,0,1:T(8,128)S(1)} %get-tuple-element.188, pred[2048]{0:T(1024)(128)(4,1)S(1)} %add_compare_fusion.2, f32[64,2,8]{2,0,1:T(8,128)S(1)} %copy.106), kind=kOutput, calls=%fused_computation.16.clone.1 | convolution fusion | flops 547618816 | bytes 9709568 | tf_op jit(solution)/shard_map/while/body/eval_jaxpr/tkgs,skd->tkgd/dot_general | solution.py:31
  72.3 0.8 bitcast_dynamic-update-slice_fusion.2
  73.1 0.7 add_compare_fusion.2
  73.8 2.4 %bitcast_reduce_fusion.2 = (f32[64,2,8]{2,0,1:T(8,128)S(1)}, f32[2,64,8,2048]{3,2,1,0:T(8,128)S(1)}) fusion(pred[2048]{0:T(1024)(128)(4,1)S(1)} %add_compare_fusion.2, bf16[2048,2,128]{2,0,1:T(8,128)(2,1)S(1)} %get-tuple-element.215, bf16[4,64,2,8,128]{4,3,2,1,0:T(8,128)(2,1)} %get-tuple-element.214, s32[]{:T(128)} %get-tuple-element.201), kind=kOutput, calls=%fused_computation.2.clone.1 | convolution fusion | flops 543161344 | bytes 9705984 | tf_op jit(solution)/shard_map/while/body/eval_jaxpr/tkgd,skd->tkgs/dot_general | solution.py:23
  76.2 3.2 %copy-done = f32[2,64,8,2048]{3,2,1,0:T(8,128)} copy-done((f32[2,64,8,2048]{3,2,1,0:T(8,128)}, f32[2,64,8,2048]{3,2,1,0:T(8,128)S(1)}, u32[]{:S(2)}) %copy-start) | copy-done | bytes 8388632 | tf_op jit(solution)/shard_map/while
  79.4 2.2 %fusion.57 = f32[64,2,8]{2,0,1:T(8,128)S(1)} fusion(f32[2,64,8,2048]{3,2,1,0:T(8,128)S(1)} %get-tuple-element.187, f32[64,2,8]{2,0,1:T(8,128)S(1)} %get-tuple-element.188, pred[2048]{0:T(1024)(128)(4,1)S(1)} %add_compare_fusion.2), kind=kLoop, calls=%fused_computation.6.clone.1 | loop fusion | flops 10484736 | bytes 8398848 | tf_op jit(solution)/shard_map/while/body/eval_jaxpr/reduce_sum | solution.py:30
  81.8 0.1 copy.106
  81.9 5.1 %fusion.58 = bf16[64,2,8,128]{3,2,0,1:T(8,128)(2,1)S(1)} fusion(bf16[2048,2,128]{2,0,1:T(8,128)(2,1)S(1)} %get-tuple-element.216, f32[2,64,8,2048]{3,2,1,0:T(8,128)} %copy-done, f32[64,2,8]{2,0,1:T(8,128)S(1)} %get-tuple-element.188, pred[2048]{0:T(1024)(128)(4,1)S(1)} %add_compare_fusion.2, f32[64,2,8]{2,0,1:T(8,128)S(1)} %copy.106), kind=kOutput, calls=%fused_computation.16.clone.1 | convolution fusion | flops 547618816 | bytes 9709568 | tf_op jit(solution)/shard_map/while/body/eval_jaxpr/tkgs,skd->tkgd/dot_general | solution.py:31
  87.0 0.8 bitcast_dynamic-update-slice_fusion.2
  87.8 0.1 broadcast_in_dim_reshape.7
  88.1 0.2 collective-permute-start
  88.3 0.4 convolution_bitcast_fusion
  88.7 1.7 %collective-permute-start.1 = (f32[1,64,16]{1,2,0:T(8,128)S(1)}, f32[1,64,16]{1,2,0:T(8,128)S(1)}, u32[]{:S(2)}, u32[]{:S(2)}) collective-permute-start(f32[1,64,16]{1,2,0:T(8,128)S(1)} %get-tuple-element.130), channel_id=1, source_target_pairs={{0,8},{4,12},{8,0},{12,4},{1,9},{5,13},{9,1},{13,5},{2,10},{6,14},... | collective-permute-start | bytes 12296 | tf_op jit(solution)/shard_map/ppermute | solution.py:17
  90.4 3.5 %all-to-all-start = ((bf16[1,256,16,128]{3,2,0,1:T(8,128)(2,1)}), bf16[1,256,16,128]{3,2,0,1:T(8,128)(2,1)S(1)}, u32[]{:S(2)}, u32[]{:S(2)}) async-start(bf16[1,256,16,128]{3,2,0,1:T(8,128)(2,1)} %bitcast.120), calls=%async_computation | async-start | bytes 2097152 | tf_op jit(solution)/shard_map/all_to_all | solution.py:70
  94.3 0.6 copy.75
  94.9 13.4 %all-to-all-done = bf16[1,256,16,128]{3,2,0,1:T(8,128)(2,1)S(1)} async-done(((bf16[1,256,16,128]{3,2,0,1:T(8,128)(2,1)}), bf16[1,256,16,128]{3,2,0,1:T(8,128)(2,1)S(1)}, u32[]{:S(2)}, u32[]{:S(2)}) %all-to-all-start) | async-done | bytes 1048608 | tf_op jit(solution)/shard_map/all_to_all | solution.py:70
  108.3 1.3 %fusion.31 = f32[64,16,1,128]{3,2,1,0:T(1,128)S(1)} fusion(bf16[4,64,16,1]{0,3,2,1:T(2,128)(2,1)S(1)} %copy.75, bf16[4,64,16,128]{3,2,1,0:T(8,128)(2,1)S(1)} %bitcast.119), kind=kOutput, calls=%fused_computation.31 | convolution fusion | flops 1048576 | bytes 1581056 | tf_op jit(solution)/shard_map/sthd,sth->thd/dot_general | solution.py:74
  109.7 1.1 fusion.37
  (46 shorter events, 1.3 us)
Async XLA Ops:
  6.5 22.5 %all-gather.2.cloned.1.call-start = ((), (), s32[]{:S(2)}) async-start(), calls=%async_computation.1 | async-start | bytes 1310720 | tf_op jit(solution)/shard_map/all_gather | solution.py:44
  32.1 3.2 %copy-start = (f32[2,64,8,2048]{3,2,1,0:T(8,128)}, f32[2,64,8,2048]{3,2,1,0:T(8,128)S(1)}, u32[]{:S(2)}) copy-start(f32[2,64,8,2048]{3,2,1,0:T(8,128)S(1)} %get-tuple-element.187) | copy-start | bytes 25165828 | tf_op jit(solution)/shard_map/while
  46.8 3.2 %copy-start = (f32[2,64,8,2048]{3,2,1,0:T(8,128)}, f32[2,64,8,2048]{3,2,1,0:T(8,128)S(1)}, u32[]{:S(2)}) copy-start(f32[2,64,8,2048]{3,2,1,0:T(8,128)S(1)} %get-tuple-element.187) | copy-start | bytes 25165828 | tf_op jit(solution)/shard_map/while
  61.5 3.2 %copy-start = (f32[2,64,8,2048]{3,2,1,0:T(8,128)}, f32[2,64,8,2048]{3,2,1,0:T(8,128)S(1)}, u32[]{:S(2)}) copy-start(f32[2,64,8,2048]{3,2,1,0:T(8,128)S(1)} %get-tuple-element.187) | copy-start | bytes 25165828 | tf_op jit(solution)/shard_map/while
  76.2 3.2 %copy-start = (f32[2,64,8,2048]{3,2,1,0:T(8,128)}, f32[2,64,8,2048]{3,2,1,0:T(8,128)S(1)}, u32[]{:S(2)}) copy-start(f32[2,64,8,2048]{3,2,1,0:T(8,128)S(1)} %get-tuple-element.187) | copy-start | bytes 25165828 | tf_op jit(solution)/shard_map/while
  88.1 5.9 %collective-permute-start = (f32[1,64,16]{1,2,0:T(8,128)S(1)}, f32[1,64,16]{1,2,0:T(8,128)S(1)}, u32[]{:S(2)}, u32[]{:S(2)}) collective-permute-start(f32[1,64,16]{1,2,0:T(8,128)S(1)} %get-tuple-element.131), channel_id=1, source_target_pairs={{0,12},{4,0},{8,4},{12,8},{1,13},{5,1},{9,5},{13,9},{2,14},{6,2},{... | collective-permute-start | bytes 12296 | tf_op jit(solution)/shard_map/ppermute | solution.py:17
  88.7 5.3 %collective-permute-start.1 = (f32[1,64,16]{1,2,0:T(8,128)S(1)}, f32[1,64,16]{1,2,0:T(8,128)S(1)}, u32[]{:S(2)}, u32[]{:S(2)}) collective-permute-start(f32[1,64,16]{1,2,0:T(8,128)S(1)} %get-tuple-element.130), channel_id=1, source_target_pairs={{0,8},{4,12},{8,0},{12,4},{1,9},{5,13},{9,1},{13,5},{2,10},{6,14},... | collective-permute-start | bytes 12296 | tf_op jit(solution)/shard_map/ppermute | solution.py:17
  90.4 3.6 %collective-permute-start.2 = (f32[1,64,16]{1,2,0:T(8,128)S(1)}, f32[1,64,16]{1,2,0:T(8,128)S(1)}, u32[]{:S(2)}, u32[]{:S(2)}) collective-permute-start(f32[1,64,16]{1,2,0:T(8,128)S(1)} %get-tuple-element.129), channel_id=1, source_target_pairs={{0,4},{4,8},{8,12},{12,0},{1,5},{5,9},{9,13},{13,1},{2,6},{6,10},{... | collective-permute-start | bytes 12296 | tf_op jit(solution)/shard_map/ppermute | solution.py:17
  90.4 17.9 %all-to-all-start = ((bf16[1,256,16,128]{3,2,0,1:T(8,128)(2,1)}), bf16[1,256,16,128]{3,2,0,1:T(8,128)(2,1)S(1)}, u32[]{:S(2)}, u32[]{:S(2)}) async-start(bf16[1,256,16,128]{3,2,0,1:T(8,128)(2,1)} %bitcast.120), calls=%async_computation | async-start | bytes 2097152 | tf_op jit(solution)/shard_map/all_to_all | solution.py:70
Sparse Core Ops, SparseCore 0:
  8.9 20.1 all-gather.1
